TPU v7x, 1024 devices: a whole 4x4x32 slice. The times are simulated.
1024 devices in a mesh: chan: 32 (over y, z_lo), ctx: 32 (over z_hi, x, core).
Axes of the slice: x: 4, y: 4, z: 32 (z_hi: 4, z_lo: 8; z = z_hi * 8 + z_lo), core: 2. Of those that a mesh axis runs over, the one named last changes fastest.
Arguments:
- key_proj: bfloat16 [32768, 4096], P('ctx', 'chan'), may hold values from -6 to 6
- value_proj: bfloat16 [32768, 4096], P('ctx', 'chan'), may hold values from -6 to 6
- query_proj: bfloat16 [32768, 4096], P('ctx', 'chan'), may hold values from -6 to 6
- short_filter: bfloat16 [3, 3, 4096], P(None, None, 'chan'), may hold values from -3.5 to 3.5
- decay_rate: float32 [16, 4096], P(None, 'chan'), may hold values from 1.5258789e-05 to 0.05
- residue: float32 [16, 4096], P(None, 'chan'), may hold values from -0.03 to 0.03
- skip_gain: float32 [4096], P('chan'), may hold values from -1 to 1
- out_weight: bfloat16 [4096, 4096], P('chan'), may hold values from -0.1875 to 0.1875
Outputs:
- block_out: bfloat16 [32768, 4096], P('ctx', 'chan')
All inputs are finite; a program needn't handle non-finite values.
Results may differ from a plain program's by a relative error of at most 0.023.
Values may be sent and summed in bfloat16 or wider, within the bound.
No kernel may reach another device: no remote copies, remote signals or barrier semaphores. Data moves between devices by JAX's collectives and lax.ppermute only.
A program may use at most 64 MiB of HBM per device.

v0:
```python
from functools import partial

import jax
import jax.numpy as jnp
from jax import lax
from jax.experimental import pallas as pl
from jax.experimental.pallas import tpu as pltpu
from jax.sharding import Mesh, PartitionSpec as P


CTX = ("w", "xa", "xb", "core")
X = ("xa", "xb")
CHUNKS = 8


def features(padded, ref, tail, taps):
    rows = ref.shape[0]
    padded[6:8, :] = tail.astype(jnp.float32)
    padded[8:, :] = ref[...].astype(jnp.float32)
    total = taps[0:1, :] * padded[8 : 8 + rows, :]
    total = total + taps[1:2, :] * padded[7 : 7 + rows, :]
    return total + taps[2:3, :] * padded[6 : 6 + rows, :]


def first_pass(q, k, v, tail, taps, rates, featq, product, prefix, message, padded, signal):
    rows, chans = q.shape
    length = rows // CHUNKS
    modes = rates.shape[0]
    weights = taps[...].astype(jnp.float32)
    featq[...] = features(padded, q, tail[0], weights[0])
    last_query = padded[rows + 6 :, :]
    keyed = features(padded, k, tail[1], weights[1])
    last_key = padded[rows + 6 :, :]
    valued = features(padded, v, tail[2], weights[2])
    last_value = padded[rows + 6 :, :]
    edges = [keyed[0:2, :], valued[0:2, :], last_key, last_value, last_query]
    edges.append(jnp.zeros((6, chans), jnp.float32))
    prod = (keyed * valued).astype(jnp.bfloat16).astype(jnp.float32)
    product[...] = prod
    signal[...] = prod
    decay = [
        jnp.broadcast_to(jnp.exp(-rates[m : m + 1, :]), (CHUNKS, chans)) for m in range(modes)
    ]

    def step(t, held):
        row = signal[pl.ds(t, CHUNKS, stride=length), :]
        return tuple(decay[m] * held[m] + row for m in range(modes))

    zero = jnp.zeros((CHUNKS, chans), jnp.float32)
    held = lax.fori_loop(0, length, step, (zero,) * modes, unroll=4)
    index = lax.broadcasted_iota(jnp.int32, (CHUNKS, chans), 0)
    left = []
    for m in range(modes):
        rate = rates[m : m + 1, :]
        run = held[m]
        reach = 1
        while reach < CHUNKS:
            before = jnp.where(index >= reach, pltpu.roll(run, reach, 0), 0.0)
            run = run + jnp.exp(-rate * float(length * reach)) * before
            reach *= 2
        prefix[m] = jnp.where(index >= 1, pltpu.roll(run, 1, 0), 0.0)
        left.append(run[CHUNKS - 1 :, :])
    message[...] = jnp.concatenate(left + edges, axis=0)


def joined(rates, own, *rest, axis, span):
    *others, out, before = rest
    values = [own[...]] + [o[...] for o in others]
    modes = rates.shape[0]
    count = len(values)
    here = lax.axis_index(axis)
    decay = jnp.exp(-rates[...] * float(span))
    total = ahead = jnp.zeros(rates.shape, jnp.float32)
    ends = []
    for i in range(count):
        value = values[0]
        for d in range(1, count):
            value = jnp.where(lax.rem(here - d + count, count) == i, values[d], value)
        ends.append(value)
        ahead = jnp.where(i < here, decay * ahead + value[0:modes, :], ahead)
        total = decay * total + value[0:modes, :]
    row = lax.broadcasted_iota(jnp.int32, own.shape, 0)
    edges = jnp.where(row < modes + 4, ends[0], ends[-1])
    out[...] = jnp.concatenate([total, edges[modes:, :]], axis=0)
    before[...] = ahead


def edge_change(message, before, taps, modes):
    def pair(head, tail, weights):
        old0 = message[modes + head : modes + head + 1, :]
        old1 = message[modes + head + 1 : modes + head + 2, :]
        back2 = before[modes + tail : modes + tail + 1, :]
        back1 = before[modes + tail + 1 : modes + tail + 2, :]
        new0 = (old0 + weights[1:2, :] * back1) + weights[2:3, :] * back2
        return old0, old1, new0, old1 + weights[2:3, :] * back1

    def rounded(value):
        return value.astype(jnp.bfloat16).astype(jnp.float32)

    k0, k1, kn0, kn1 = pair(0, 4, taps[1])
    v0, v1, vn0, vn1 = pair(2, 6, taps[2])
    return rounded(kn0 * vn0) - rounded(k0 * v0), rounded(kn1 * vn1) - rounded(k1 * v1)


def second_pass(
    featq, product, prefix, low, mid, high, own, back1, back2, back3,
    taps, rates, residue, gain, gated, signal, mixed,
):
    rows, chans = product.shape
    length = rows // CHUNKS
    modes = rates.shape[0]
    core, xb, xa = (lax.axis_index(a) for a in ("core", "xb", "xa"))
    two = rows * lax.axis_size("core")
    four = two * lax.axis_size("xb")
    run = four * lax.axis_size("xa")
    rate = rates[...]
    weights = taps[...].astype(jnp.float32)

    def power(tokens):
        return jnp.exp(-rate * tokens)

    chain = [own[...], back1[...], back2[...], back3[...], jnp.zeros(own.shape, jnp.float32)]
    start = jnp.zeros((modes, chans), jnp.float32)
    whole = power(float(run))
    for d in (3, 2, 1):
        first, second = edge_change(chain[d], chain[d + 1], weights, modes)
        total = chain[d][0:modes, :] + power(run - 1.0) * first + power(run - 2.0) * second
        start = whole * start + total
    first, second = edge_change(chain[0], chain[1], weights, modes)
    lost = jnp.exp(rate) * first + jnp.exp(2.0 * rate) * second
    ahead = (core * rows + xb * two + xa * four).astype(jnp.float32)
    leads = ahead < 1.0
    carried = start + jnp.where(leads, 0.0, lost)
    for part, place, span in ((high, xa, four), (mid, xb, two), (low, core, rows)):
        carried = part[...] + power(place.astype(jnp.float32) * float(span)) * carried
    lost = jnp.where(leads, lost, 0.0)

    wide = (CHUNKS, chans)
    row = lax.broadcasted_iota(jnp.int32, wide, 0)
    index = row.astype(jnp.float32)
    dp0, dp1 = jnp.where(leads, first, 0.0), jnp.where(leads, second, 0.0)
    signal[...] = product[...]
    signal[0:CHUNKS, :] = product[0:CHUNKS, :] + jnp.where(
        row == 0, dp0, jnp.where(row == 1, dp1, 0.0)
    )
    held = []
    decay = []
    weight = []
    for m in range(modes):
        one = rate[m : m + 1, :]
        decay.append(jnp.broadcast_to(jnp.exp(-one), wide))
        weight.append(jnp.broadcast_to(residue[m : m + 1, :], wide))
        reach = jnp.exp(-one * (index * float(length)))
        before = carried[m : m + 1, :] + jnp.where(row >= 1, lost[m : m + 1, :], 0.0)
        held.append(prefix[m] + reach * before)

    def step(t, held):
        now = signal[pl.ds(t, CHUNKS, stride=length), :]
        held = tuple(decay[m] * held[m] + now for m in range(modes))
        terms = [weight[m] * held[m] for m in range(modes)]
        while len(terms) > 1:
            terms = [terms[i] + terms[i + 1] for i in range(0, len(terms), 2)]
        mixed[pl.ds(t, CHUNKS, stride=length), :] = terms[0]
        return held

    lax.fori_loop(0, length, step, tuple(held), unroll=2)
    long_out = (mixed[...] + gain[...] * signal[...]).astype(jnp.bfloat16).astype(jnp.float32)
    gated[...] = (featq[...] * long_out).astype(jnp.bfloat16)
    last2 = back1[modes + 8 : modes + 9, :]
    last1 = back1[modes + 9 : modes + 10, :]
    top = lax.broadcasted_iota(jnp.int32, (16, chans), 0)
    dq0 = jnp.where(leads, weights[0][1:2, :] * last1 + weights[0][2:3, :] * last2, 0.0)
    dq1 = jnp.where(leads, weights[0][2:3, :] * last1, 0.0)
    query = featq[0:16, :] + jnp.where(top == 0, dq0, jnp.where(top == 1, dq1, 0.0))
    gated[0:16, :] = (query * long_out[0:16, :]).astype(jnp.bfloat16)


def project(gathered, mine, other, shares):
    ny, nb = gathered.shape[:2]
    nx = mine.shape[0]
    core = lax.axis_index("core")
    width = shares.shape[2]

    def run(halves):
        left = jnp.concatenate([gathered[i, j] for i in range(ny) for j in range(nb)], axis=1)
        for n in range(0, shares.shape[0], 2):
            cols = slice(n * width, (n + 2) * width)
            right = jnp.concatenate(
                [
                    half[x, i, j, :, cols]
                    for i in range(ny)
                    for j in range(nb)
                    for x in range(nx)
                    for half in halves
                ],
                axis=0,
            )
            both = jnp.dot(left, right, preferred_element_type=jnp.float32).astype(shares.dtype)
            shares[n] = both[:, :width]
            shares[n + 1] = both[:, width:]

    @pl.when(core == 0)
    def _():
        run((mine, other))

    @pl.when(core == 1)
    def _():
        run((other, mine))


def moved(value, axis, pairs):
    return lax.ppermute(value, axis, pairs)


def near_vmem(value):
    return pltpu.with_memory_space_constraint(value, pltpu.VMEM)


def everyone(value, axis):
    count = lax.axis_size(axis)
    return lax.all_to_all(
        jnp.broadcast_to(value[None], (count,) + value.shape), axis, 0, 0, tiled=True
    )


def own_weights(out_weight):
    ny, nb = lax.axis_size("y"), lax.axis_size("zb")
    ncore = lax.axis_size("core")
    share = out_weight.shape[0] // (lax.axis_size(X) * ncore)
    first = (lax.axis_index(X) * ncore + lax.axis_index("core")) * share
    rows = lax.dynamic_slice_in_dim(out_weight, first, share, 0)
    blocks = rows.reshape(share, ny, -1).transpose(1, 0, 2)
    blocks = jnp.broadcast_to(blocks[:, None], (ny, nb) + blocks.shape[1:])
    blocks = blocks.reshape((ny * nb,) + blocks.shape[2:])
    got = lax.all_to_all(blocks, ("y", "zb"), 0, 0, tiled=True)
    return got.reshape((ny, nb) + got.shape[1:])


def layer(
    key_proj, value_proj, query_proj, short_filter, decay_rate, residue, skip_gain, out_weight
):
    rows, chans = key_proj.shape
    modes = decay_rate.shape[0]
    na, nb = lax.axis_size("za"), lax.axis_size("zb")
    ncore, nx, nw = (lax.axis_size(a) for a in ("core", X, "w"))
    f32 = jnp.float32
    weights = own_weights(out_weight)
    tails = jnp.stack([query_proj[rows - 2 :], key_proj[rows - 2 :], value_proj[rows - 2 :]], 0)
    near = [(i, i + 1) for i in range(nw * nx * ncore - 1) if (i + 1) % (nx * ncore) > 0]
    tails = moved(tails, CTX, near)
    featq, product, prefix, message = pl.pallas_call(
        first_pass,
        out_shape=(
            jax.ShapeDtypeStruct((rows, chans), f32),
            jax.ShapeDtypeStruct((rows, chans), f32),
            jax.ShapeDtypeStruct((modes, CHUNKS, chans), f32),
            pltpu.VMEM((modes + 16, chans), f32),
        ),
        in_specs=[pl.BlockSpec(memory_space=pltpu.VMEM)] * 6,
        out_specs=(pl.BlockSpec(memory_space=pltpu.VMEM),) * 4,
        scratch_shapes=[pltpu.VMEM((rows + 8, chans), f32), pltpu.VMEM((rows, chans), f32)],
        name="first_pass",
    )(query_proj, key_proj, value_proj, near_vmem(tails), short_filter, decay_rate)

    def join(value, axis, span):
        count = lax.axis_size(axis)
        rest = [
            moved(value, axis, [(i, (i + d) % count) for i in range(count)])
            for d in range(1, count)
        ]
        return pl.pallas_call(
            partial(joined, axis=axis, span=span),
            out_shape=(
                pltpu.VMEM((modes + 16, chans), f32),
                pltpu.VMEM((modes, chans), f32),
            ),
            in_specs=[pl.BlockSpec(memory_space=pltpu.VMEM)] * (count + 1),
            out_specs=(pl.BlockSpec(memory_space=pltpu.VMEM),) * 2,
        )(decay_rate, near_vmem(value), *[near_vmem(r) for r in rest])

    message, low = join(message, "core", rows)
    message, mid = join(message, "xb", rows * ncore)
    own, high = join(message, "xa", rows * ncore * lax.axis_size("xb"))
    back = {}
    back[1] = moved(own, "w", [(i, i + 1) for i in range(nw - 1)])
    back[3] = moved(own, "w", [(0, nw - 1)])
    weights = everyone(weights, X)
    held = jnp.where(lax.axis_index("w") == nw - 1, back[3], back[1])
    back[2] = moved(held, "w", [(nw - 2, nw - 1), (nw - 1, nw - 2)])
    gated = pl.pallas_call(
        second_pass,
        out_shape=jax.ShapeDtypeStruct((rows, chans), jnp.bfloat16),
        scratch_shapes=[pltpu.VMEM((rows, chans), f32), pltpu.VMEM((rows, chans), f32)],
        in_specs=[pl.BlockSpec(memory_space=pltpu.VMEM)] * 14,
        out_specs=pl.BlockSpec(memory_space=pltpu.VMEM),
        name="second_pass",
    )(
        featq, product, prefix, *[near_vmem(v) for v in (low, mid, high, own)],
        *[near_vmem(back[d]) for d in (1, 2, 3)],
        short_filter, decay_rate, residue, skip_gain[None],
    )
    other = moved(weights, "core", [(0, 1), (1, 0)])
    quarter = rows // nb
    mine = lax.all_to_all(gated.reshape(nb, quarter, chans), "zb", 0, 0, tiled=True)
    gathered = everyone(mine, "y")
    shares = pl.pallas_call(
        project,
        out_shape=jax.ShapeDtypeStruct((na * nb, quarter, chans), jnp.bfloat16),
        name="project",
    )(gathered, weights, other)
    parts = lax.all_to_all(shares, ("za", "zb"), 0, 0, tiled=True)
    total = parts.reshape(na, rows, chans).astype(f32).sum(0)
    return total.astype(jnp.bfloat16)


def solution(mesh):
    fine = Mesh(mesh.devices.reshape(4, 2, 4, 4, 2, 2, 2), ("y", "za", "zb") + CTX)
    chan = ("y", "za", "zb")
    placed = (
        P(CTX, chan),
        P(CTX, chan),
        P(CTX, chan),
        P(None, None, chan),
        P(None, chan),
        P(None, chan),
        P(chan),
        P(chan, None),
    )
    return jax.shard_map(layer, mesh=fine, in_specs=placed, out_specs=P(CTX, chan), check_vma=False)
```

profile of v0, /device:TPU:774, one launch (start us, length us, event | category | flops | bytes accessed | tf_op | source)
XLA Modules:
  0.0 169.0 jit_solution(3406322489138285599)
XLA Ops:
  0.0 1.2 copy-done
  1.4 22.2 %all_to_all.25 = bf16[16,16,1024]{2,1,0:T(8,128)(2,1)S(1)} all-to-all(bf16[16,16,1024]{2,1,0:T(8,128)(2,1)S(1)} %bitcast.15), channel_id=1, replica_groups=mesh['y'=4,'za'=2,'zb'=4,'w'=4,'xa'=2,'xb'=2,'core'=2] {'y','zb'}, dimensions={0} | all-to-all | bytes 1048576 | tf_op jit(solution)/shard_map/all_to_all | solution.py:235
  23.7 1.6 broadcast_in_dim.26
  25.3 4.8 %all-to-all-start.3 = ((bf16[4,4,4,16,1024]{4,3,2,1,0:T(8,128)(2,1)}), bf16[4,4,4,16,1024]{4,3,2,1,0:T(8,128)(2,1)S(1)}, u32[]{:S(2)}, u32[]{:S(2)}) async-start(bf16[4,4,4,16,1024]{4,3,2,1,0:T(8,128)(2,1)} %broadcast_in_dim.26), calls=%async_computation.3 | async-start | bytes 4194304 | tf_op jit(solution)/shard_map/all_to_all | solution.py:221
  31.4 1.9 %collective-permute-start = (bf16[3,2,128]{2,1,0:T(2,128)(2,1)S(1)}, bf16[3,2,128]{2,1,0:T(2,128)(2,1)S(1)}, u32[]{:S(2)}, u32[]{:S(2)}) collective-permute-start(bf16[3,2,128]{2,1,0:T(2,128)(2,1)S(1)} %pad_maximum_fusion), channel_id=1, source_target_pairs={{0,1},{1,2},{2,3},{3,4},{4,5},{5,6},{6,7},{8,9},{9,10},{10,11},{11... | collective-permute-start | bytes 4616 | tf_op jit(solution)/shard_map/ppermute | solution.py:212
  33.4 16.9 %collective-permute-done.tail = bf16[3,2,128]{2,1,0:T(2,128)(2,1)S(1)} collective-permute-done((bf16[3,2,128]{2,1,0:T(2,128)(2,1)S(1)}, bf16[3,2,128]{2,1,0:T(2,128)(2,1)S(1)}, u32[]{:S(2)}, u32[]{:S(2)}) %collective-permute-start) | collective-permute-done | bytes 1568 | tf_op jit(solution)/shard_map/ppermute | solution.py:212
  50.3 3.8 %first_pass.1 = (f32[1024,128]{1,0:T(8,128)}, f32[1024,128]{1,0:T(8,128)}, f32[16,8,128]{2,1,0:T(8,128)}, f32[32,128]{1,0:T(8,128)S(1)}) custom-call(bf16[1024,128]{1,0:T(8,128)(2,1)} %q.1, bf16[1024,128]{1,0:T(8,128)(2,1)} %k.1, bf16[1024,128]{1,0:T(8,128)(2,1)} %v.1, bf16[3,2,128]{2,1,0:T(2,128)(2,1)S(1)} %collective-permute-done.tail, ...), custom_call_target="tpu_custom_call" | custom-call | tf_op jit(solution)/shard_map/first_pass/pallas_call | solution.py:251
  54.1 1.9 %collective-permute-start.1 = (f32[32,128]{1,0:T(8,128)S(1)}, f32[32,128]{1,0:T(8,128)S(1)}, u32[]{:S(2)}, u32[]{:S(2)}) collective-permute-start(f32[32,128]{1,0:T(8,128)S(1)} %get-tuple-element.18.own), channel_id=1, source_target_pairs={{0,1},{1,0},{2,3},{3,2},{4,5},{5,4},{6,7},{7,6},{8,9},{9,8},{10,11... | collective-permute-start | bytes 49160 | tf_op jit(solution)/shard_map/ppermute | solution.py:212
  57.9 1.9 %collective-permute-start.2 = (f32[32,128]{1,0:T(8,128)S(1)}, f32[32,128]{1,0:T(8,128)S(1)}, u32[]{:S(2)}, u32[]{:S(2)}) collective-permute-start(f32[32,128]{1,0:T(8,128)S(1)} %get-tuple-element.20.own), channel_id=1, source_target_pairs={{0,2},{2,0},{1,3},{3,1},{4,6},{6,4},{5,7},{7,5},{8,10},{10,8},{9,1... | collective-permute-start | bytes 49160 | tf_op jit(solution)/shard_map/ppermute | solution.py:212
  59.8 3.7 %collective-permute-done.2.rest_0_ = f32[32,128]{1,0:T(8,128)S(1)} collective-permute-done((f32[32,128]{1,0:T(8,128)S(1)}, f32[32,128]{1,0:T(8,128)S(1)}, u32[]{:S(2)}, u32[]{:S(2)}) %collective-permute-start.2) | collective-permute-done | bytes 16416 | tf_op jit(solution)/shard_map/ppermute | solution.py:212
  64.2 3.1 %collective-permute-start.3 = (f32[32,128]{1,0:T(8,128)S(1)}, f32[32,128]{1,0:T(8,128)S(1)}, u32[]{:S(2)}, u32[]{:S(2)}) collective-permute-start(f32[32,128]{1,0:T(8,128)S(1)} %get-tuple-element.22.own), channel_id=1, source_target_pairs={{0,4},{4,0},{1,5},{5,1},{2,6},{6,2},{3,7},{7,3},{8,12},{12,8},{9,1... | collective-permute-start | bytes 49160 | tf_op jit(solution)/shard_map/ppermute | solution.py:212
  67.3 4.0 %collective-permute-done.3.rest_0_ = f32[32,128]{1,0:T(8,128)S(1)} collective-permute-done((f32[32,128]{1,0:T(8,128)S(1)}, f32[32,128]{1,0:T(8,128)S(1)}, u32[]{:S(2)}, u32[]{:S(2)}) %collective-permute-start.3) | collective-permute-done | bytes 16416 | tf_op jit(solution)/shard_map/ppermute | solution.py:212
  72.1 1.3 collective-permute-start.5
  73.4 1.3 collective-permute-start.4
  74.7 11.9 %collective-permute-done.5.back3 = f32[32,128]{1,0:T(8,128)S(1)} collective-permute-done((f32[32,128]{1,0:T(8,128)S(1)}, f32[32,128]{1,0:T(8,128)S(1)}, u32[]{:S(2)}, u32[]{:S(2)}) %collective-permute-start.5) | collective-permute-done | bytes 16416 | tf_op jit(solution)/shard_map/ppermute | solution.py:212
  87.7 7.8 %collective-permute-start.6 = (f32[32,128]{1,0:T(8,128)S(1)}, f32[32,128]{1,0:T(8,128)S(1)}, u32[]{:S(2)}, u32[]{:S(2)}) collective-permute-start(f32[32,128]{1,0:T(8,128)S(1)} %broadcast_select_fusion), channel_id=1, source_target_pairs={{16,24},{24,16},{17,25},{25,17},{18,26},{26,18},{19,27},{27,19},{2... | collective-permute-start | bytes 49160 | tf_op jit(solution)/shard_map/ppermute | solution.py:212
  95.6 6.5 %collective-permute-done.6.back2 = f32[32,128]{1,0:T(8,128)S(1)} collective-permute-done((f32[32,128]{1,0:T(8,128)S(1)}, f32[32,128]{1,0:T(8,128)S(1)}, u32[]{:S(2)}, u32[]{:S(2)}) %collective-permute-start.6) | collective-permute-done | bytes 16416 | tf_op jit(solution)/shard_map/ppermute | solution.py:212
  102.1 4.2 %second_pass.1 = bf16[1024,128]{1,0:T(8,128)(2,1)} custom-call(f32[1024,128]{1,0:T(8,128)} %get-tuple-element.15.featq, f32[1024,128]{1,0:T(8,128)} %get-tuple-element.16.product, f32[16,8,128]{2,1,0:T(8,128)} %get-tuple-element.17.prefix, f32[16,128]{1,0:T(8,128)S(1)} %get-tuple-element.19.low, f32[16,128]{1,0:T(8,128)S(1)} %get-tuple-element.21.mid, ...), custom_call_target="tpu_custom_call" | custom-call | tf_op jit(solution)/shard_map/second_pass/pallas_call | solution.py:290
  106.2 3.4 %all-to-all-start = ((bf16[4,256,128]{2,1,0:T(8,128)(2,1)}), bf16[4,256,128]{2,1,0:T(8,128)(2,1)S(1)}, u32[]{:S(2)}, u32[]{:S(2)}) async-start(bf16[4,256,128]{2,1,0:T(8,128)(2,1)} %bitcast.17), calls=%async_computation | async-start | bytes 524288 | tf_op jit(solution)/shard_map/all_to_all | solution.py:304
  109.7 1.9 %collective-permute-start.7 = (bf16[4,4,4,16,1024]{4,3,2,1,0:T(8,128)(2,1)S(1)}, bf16[4,4,4,16,1024]{4,3,2,1,0:T(8,128)(2,1)}, u32[]{:S(2)}, u32[]{:S(2)}) collective-permute-start(bf16[4,4,4,16,1024]{4,3,2,1,0:T(8,128)(2,1)S(1)} %all-to-all-done.3.mine), channel_id=1, source_target_pairs={{0,1},{1,0},{2,3},{3,2},{4,5},{5,4},{6,7},{7,6},{8,9},{9,8},{10,11... | collective-permute-start | bytes 6291464 | tf_op jit(solution)/shard_map/ppermute | solution.py:212
  111.6 4.8 %all-to-all-done = bf16[4,256,128]{2,1,0:T(8,128)(2,1)S(1)} async-done(((bf16[4,256,128]{2,1,0:T(8,128)(2,1)}), bf16[4,256,128]{2,1,0:T(8,128)(2,1)S(1)}, u32[]{:S(2)}, u32[]{:S(2)}) %all-to-all-start) | async-done | bytes 262176 | tf_op jit(solution)/shard_map/all_to_all | solution.py:304
  116.6 14.4 %all_to_all.26.gathered = bf16[4,4,256,128]{3,2,1,0:T(8,128)(2,1)} all-to-all(bf16[4,4,256,128]{3,2,1,0:T(8,128)(2,1)S(1)} %broadcast_in_dim.11), channel_id=1, replica_groups=mesh['y'=4,'za'=2,'zb'=4,'w'=4,'xa'=2,'xb'=2,'core'=2] {'y'}, dimensions={0} | all-to-all | bytes 2097152 | tf_op jit(solution)/shard_map/all_to_all | solution.py:221
  131.0 4.6 %project.1 = bf16[8,256,128]{2,1,0:T(8,128)(2,1)} custom-call(bf16[4,4,256,128]{3,2,1,0:T(8,128)(2,1)} %all_to_all.26.gathered, bf16[4,4,4,16,1024]{4,3,2,1,0:T(8,128)(2,1)} %copy-done.1, bf16[4,4,4,16,1024]{4,3,2,1,0:T(8,128)(2,1)} %collective-permute-done.7.other), custom_call_target="tpu_custom_call" | custom-call | tf_op jit(solution)/shard_map/project/pallas_call | solution.py:306
  135.6 32.6 %all_to_all.27 = bf16[8,256,128]{2,1,0:T(8,128)(2,1)S(1)} all-to-all(bf16[8,256,128]{2,1,0:T(8,128)(2,1)} %project.1), channel_id=1, replica_groups=mesh['y'=4,'za'=2,'zb'=4,'w'=4,'xa'=2,'xb'=2,'core'=2] {'za','zb'}, dimensions={0} | all-to-all | bytes 1048576 | tf_op jit(solution)/shard_map/all_to_all | solution.py:311
  (20 shorter events, 7.0 us)
Async XLA Ops:
  0.0 1.2 copy-start
  25.3 81.0 %all-to-all-start.3 = ((bf16[4,4,4,16,1024]{4,3,2,1,0:T(8,128)(2,1)}), bf16[4,4,4,16,1024]{4,3,2,1,0:T(8,128)(2,1)S(1)}, u32[]{:S(2)}, u32[]{:S(2)}) async-start(bf16[4,4,4,16,1024]{4,3,2,1,0:T(8,128)(2,1)} %broadcast_in_dim.26), calls=%async_computation.3 | async-start | bytes 4194304 | tf_op jit(solution)/shard_map/all_to_all | solution.py:221
  31.4 18.8 %collective-permute-start = (bf16[3,2,128]{2,1,0:T(2,128)(2,1)S(1)}, bf16[3,2,128]{2,1,0:T(2,128)(2,1)S(1)}, u32[]{:S(2)}, u32[]{:S(2)}) collective-permute-start(bf16[3,2,128]{2,1,0:T(2,128)(2,1)S(1)} %pad_maximum_fusion), channel_id=1, source_target_pairs={{0,1},{1,2},{2,3},{3,4},{4,5},{5,6},{6,7},{8,9},{9,10},{10,11},{11... | collective-permute-start | bytes 4616 | tf_op jit(solution)/shard_map/ppermute | solution.py:212
  54.1 3.1 %collective-permute-start.1 = (f32[32,128]{1,0:T(8,128)S(1)}, f32[32,128]{1,0:T(8,128)S(1)}, u32[]{:S(2)}, u32[]{:S(2)}) collective-permute-start(f32[32,128]{1,0:T(8,128)S(1)} %get-tuple-element.18.own), channel_id=1, source_target_pairs={{0,1},{1,0},{2,3},{3,2},{4,5},{5,4},{6,7},{7,6},{8,9},{9,8},{10,11... | collective-permute-start | bytes 49160 | tf_op jit(solution)/shard_map/ppermute | solution.py:212
  57.9 5.6 %collective-permute-start.2 = (f32[32,128]{1,0:T(8,128)S(1)}, f32[32,128]{1,0:T(8,128)S(1)}, u32[]{:S(2)}, u32[]{:S(2)}) collective-permute-start(f32[32,128]{1,0:T(8,128)S(1)} %get-tuple-element.20.own), channel_id=1, source_target_pairs={{0,2},{2,0},{1,3},{3,1},{4,6},{6,4},{5,7},{7,5},{8,10},{10,8},{9,1... | collective-permute-start | bytes 49160 | tf_op jit(solution)/shard_map/ppermute | solution.py:212
  64.2 7.1 %collective-permute-start.3 = (f32[32,128]{1,0:T(8,128)S(1)}, f32[32,128]{1,0:T(8,128)S(1)}, u32[]{:S(2)}, u32[]{:S(2)}) collective-permute-start(f32[32,128]{1,0:T(8,128)S(1)} %get-tuple-element.22.own), channel_id=1, source_target_pairs={{0,4},{4,0},{1,5},{5,1},{2,6},{6,2},{3,7},{7,3},{8,12},{12,8},{9,1... | collective-permute-start | bytes 49160 | tf_op jit(solution)/shard_map/ppermute | solution.py:212
  72.1 14.5 %collective-permute-start.5 = (f32[32,128]{1,0:T(8,128)S(1)}, f32[32,128]{1,0:T(8,128)S(1)}, u32[]{:S(2)}, u32[]{:S(2)}) collective-permute-start(f32[32,128]{1,0:T(8,128)S(1)} %get-tuple-element.24.own), channel_id=1, source_target_pairs={{0,24},{1,25},{2,26},{3,27},{4,28},{5,29},{6,30},{7,31},{32,56},{3... | collective-permute-start | bytes 49160 | tf_op jit(solution)/shard_map/ppermute | solution.py:212
  73.4 14.3 %collective-permute-start.4 = (f32[32,128]{1,0:T(8,128)S(1)}, f32[32,128]{1,0:T(8,128)S(1)}, u32[]{:S(2)}, u32[]{:S(2)}) collective-permute-start(f32[32,128]{1,0:T(8,128)S(1)} %get-tuple-element.24.own), channel_id=1, source_target_pairs={{0,8},{8,16},{16,24},{1,9},{9,17},{17,25},{2,10},{10,18},{18,26},{... | collective-permute-start | bytes 49160 | tf_op jit(solution)/shard_map/ppermute | solution.py:212
  87.7 14.3 %collective-permute-start.6 = (f32[32,128]{1,0:T(8,128)S(1)}, f32[32,128]{1,0:T(8,128)S(1)}, u32[]{:S(2)}, u32[]{:S(2)}) collective-permute-start(f32[32,128]{1,0:T(8,128)S(1)} %broadcast_select_fusion), channel_id=1, source_target_pairs={{16,24},{24,16},{17,25},{25,17},{18,26},{26,18},{19,27},{27,19},{2... | collective-permute-start | bytes 49160 | tf_op jit(solution)/shard_map/ppermute | solution.py:212
  106.2 24.7 %copy-start.1 = (bf16[4,4,4,16,1024]{4,3,2,1,0:T(8,128)(2,1)}, bf16[4,4,4,16,1024]{4,3,2,1,0:T(8,128)(2,1)S(1)}, u32[]{:S(2)}) copy-start(bf16[4,4,4,16,1024]{4,3,2,1,0:T(8,128)(2,1)S(1)} %all-to-all-done.3.mine) | copy-start | bytes 6291460
  106.2 10.2 %all-to-all-start = ((bf16[4,256,128]{2,1,0:T(8,128)(2,1)}), bf16[4,256,128]{2,1,0:T(8,128)(2,1)S(1)}, u32[]{:S(2)}, u32[]{:S(2)}) async-start(bf16[4,256,128]{2,1,0:T(8,128)(2,1)} %bitcast.17), calls=%async_computation | async-start | bytes 524288 | tf_op jit(solution)/shard_map/all_to_all | solution.py:304
  109.7 21.3 %collective-permute-start.7 = (bf16[4,4,4,16,1024]{4,3,2,1,0:T(8,128)(2,1)S(1)}, bf16[4,4,4,16,1024]{4,3,2,1,0:T(8,128)(2,1)}, u32[]{:S(2)}, u32[]{:S(2)}) collective-permute-start(bf16[4,4,4,16,1024]{4,3,2,1,0:T(8,128)(2,1)S(1)} %all-to-all-done.3.mine), channel_id=1, source_target_pairs={{0,1},{1,0},{2,3},{3,2},{4,5},{5,4},{6,7},{7,6},{8,9},{9,8},{10,11... | collective-permute-start | bytes 6291464 | tf_op jit(solution)/shard_map/ppermute | solution.py:212
where the time goes:
time: 170 us; the launch traced here: 169 us
  blocking collectives  69.2 us (41%)
  waiting for transfers between devices  50.1 us (29%)
  starting transfers between devices  29.4 us (17%)
  Pallas kernels  14.7 us (9%)
  local copies, waits for them, and re-layouts  4.59 us (3%)
    ppermute x8, waiting for transfers between devices, moved(): return lax.ppermute(value, axis, pairs)  45.3 us
    all_to_all x1, blocking collectives, layer(): parts = lax.all_to_all(shares, ('za', 'zb'), 0, 0, tiled=True)  32.6 us
    all_to_all x1, blocking collectives, own_weights(): got = lax.all_to_all(blocks, ('y', 'zb'), 0, 0, tiled=True)  22.2 us
    ppermute x8, starting transfers between devices, moved(): return lax.ppermute(value, axis, pairs)  21.2 us
    all_to_all x1, blocking collectives, everyone(): lax.all_to_all(jnp.broadcast_to(value[None], (count,) + value.shape), axi...  14.4 us
    all_to_all x1, waiting for transfers between devices, layer(): lax.all_to_all(gated.reshape(nb, quarter, chans), 'zb', 0, 0, tiled=True)  4.81 us
    all_to_all x1, starting transfers between devices, everyone(): lax.all_to_all(jnp.broadcast_to(value[None], (count,) + value.shape), axi...  4.77 us
    pallas_call x1, Pallas kernels, layer(): pl.pallas_call(project, out_shape=jax.ShapeDtypeStruct((na * nb, quarter,...  4.62 us
  transfers between devices with their start and end apart: 10, of which 8 were waited for; matrix products, arithmetic and copies ran while one was open for 1% of the time, Pallas kernels for 6%

commit v1 on v0

--- a/solution.py
+++ b/solution.py
@@ -13,25 +13,25 @@
 CHUNKS = 8
 
 
-def features(padded, ref, tail, taps):
+def features(padded, ref, taps):
     rows = ref.shape[0]
-    padded[6:8, :] = tail.astype(jnp.float32)
+    padded[0:8, :] = jnp.zeros((8, ref.shape[1]), jnp.float32)
     padded[8:, :] = ref[...].astype(jnp.float32)
     total = taps[0:1, :] * padded[8 : 8 + rows, :]
     total = total + taps[1:2, :] * padded[7 : 7 + rows, :]
     return total + taps[2:3, :] * padded[6 : 6 + rows, :]
 
 
-def first_pass(q, k, v, tail, taps, rates, featq, product, prefix, message, padded, signal):
+def first_pass(q, k, v, taps, rates, featq, product, prefix, message, padded, signal):
     rows, chans = q.shape
     length = rows // CHUNKS
     modes = rates.shape[0]
     weights = taps[...].astype(jnp.float32)
-    featq[...] = features(padded, q, tail[0], weights[0])
+    featq[...] = features(padded, q, weights[0])
     last_query = padded[rows + 6 :, :]
-    keyed = features(padded, k, tail[1], weights[1])
+    keyed = features(padded, k, weights[1])
     last_key = padded[rows + 6 :, :]
-    valued = features(padded, v, tail[2], weights[2])
+    valued = features(padded, v, weights[2])
     last_value = padded[rows + 6 :, :]
     edges = [keyed[0:2, :], valued[0:2, :], last_key, last_value, last_query]
     edges.append(jnp.zeros((6, chans), jnp.float32))
@@ -63,26 +63,27 @@
     message[...] = jnp.concatenate(left + edges, axis=0)
 
 
-def joined(rates, own, *rest, axis, span):
-    *others, out, before = rest
-    values = [own[...]] + [o[...] for o in others]
+def joined(rates, taps, own, other, out, before, fix, *, axis, lower, span):
     modes = rates.shape[0]
-    count = len(values)
-    here = lax.axis_index(axis)
-    decay = jnp.exp(-rates[...] * float(span))
-    total = ahead = jnp.zeros(rates.shape, jnp.float32)
-    ends = []
-    for i in range(count):
-        value = values[0]
-        for d in range(1, count):
-            value = jnp.where(lax.rem(here - d + count, count) == i, values[d], value)
-        ends.append(value)
-        ahead = jnp.where(i < here, decay * ahead + value[0:modes, :], ahead)
-        total = decay * total + value[0:modes, :]
-    row = lax.broadcasted_iota(jnp.int32, own.shape, 0)
-    edges = jnp.where(row < modes + 4, ends[0], ends[-1])
+    rate = rates[...]
+    right_side = lax.axis_index(axis) == 1
+    left = jnp.where(right_side, other[...], own[...])
+    right = jnp.where(right_side, own[...], other[...])
+    first, second = edge_change(right, left, taps[...].astype(jnp.float32), modes)
+    total = jnp.exp(-rate * float(span)) * left[0:modes, :] + right[0:modes, :]
+    total = total + jnp.exp(-rate * (span - 1.0)) * first
+    total = total + jnp.exp(-rate * (span - 2.0)) * second
+    row = lax.broadcasted_iota(jnp.int32, left.shape, 0)
+    edges = jnp.where(row < modes + 4, left, right)
     out[...] = jnp.concatenate([total, edges[modes:, :]], axis=0)
-    before[...] = ahead
+    inside = sum((lax.axis_index(a) for a in lower), jnp.int32(0))
+    lost = jnp.exp(rate) * first + jnp.exp(2.0 * rate) * second
+    lost = jnp.where(inside > 0, lost, 0.0)
+    before[...] = jnp.where(right_side, left[0:modes, :] + lost, 0.0)
+    rows = [first, second, left[modes + 8 : modes + 10, :]]
+    rows.append(jnp.zeros((4,) + first.shape[1:], jnp.float32))
+    leads = jnp.logical_and(right_side, inside == 0)
+    fix[...] = jnp.where(leads, jnp.concatenate(rows, axis=0), 0.0)
 
 
 def edge_change(message, before, taps, modes):
@@ -103,7 +104,8 @@
 
 
 def second_pass(
-    featq, product, prefix, low, mid, high, own, back1, back2, back3,
+    featq, product, prefix, low, mid, high, fix_low, fix_mid, fix_high,
+    own, back1, back2, back3,
     taps, rates, residue, gain, gated, signal, mixed,
 ):
     rows, chans = product.shape
@@ -133,12 +135,15 @@
     carried = start + jnp.where(leads, 0.0, lost)
     for part, place, span in ((high, xa, four), (mid, xb, two), (low, core, rows)):
         carried = part[...] + power(place.astype(jnp.float32) * float(span)) * carried
-    lost = jnp.where(leads, lost, 0.0)
+    far = jnp.concatenate([first, second, back1[modes + 8 : modes + 10, :]], axis=0)
+    fix = fix_low[...] + fix_mid[...] + fix_high[...]
+    fix = fix[0:4, :] + jnp.where(leads, far, 0.0)
+    dp0, dp1, last2, last1 = (fix[i : i + 1, :] for i in range(4))
+    lost = jnp.exp(rate) * dp0 + jnp.exp(2.0 * rate) * dp1
 
     wide = (CHUNKS, chans)
     row = lax.broadcasted_iota(jnp.int32, wide, 0)
     index = row.astype(jnp.float32)
-    dp0, dp1 = jnp.where(leads, first, 0.0), jnp.where(leads, second, 0.0)
     signal[...] = product[...]
     signal[0:CHUNKS, :] = product[0:CHUNKS, :] + jnp.where(
         row == 0, dp0, jnp.where(row == 1, dp1, 0.0)
@@ -166,46 +171,46 @@
     lax.fori_loop(0, length, step, tuple(held), unroll=2)
     long_out = (mixed[...] + gain[...] * signal[...]).astype(jnp.bfloat16).astype(jnp.float32)
     gated[...] = (featq[...] * long_out).astype(jnp.bfloat16)
-    last2 = back1[modes + 8 : modes + 9, :]
-    last1 = back1[modes + 9 : modes + 10, :]
     top = lax.broadcasted_iota(jnp.int32, (16, chans), 0)
-    dq0 = jnp.where(leads, weights[0][1:2, :] * last1 + weights[0][2:3, :] * last2, 0.0)
-    dq1 = jnp.where(leads, weights[0][2:3, :] * last1, 0.0)
+    dq0 = weights[0][1:2, :] * last1 + weights[0][2:3, :] * last2
+    dq1 = weights[0][2:3, :] * last1
     query = featq[0:16, :] + jnp.where(top == 0, dq0, jnp.where(top == 1, dq1, 0.0))
     gated[0:16, :] = (query * long_out[0:16, :]).astype(jnp.bfloat16)
 
 
-def project(gathered, mine, other, shares):
+def project(gathered, mine, other, shares, buffer, sems):
     ny, nb = gathered.shape[:2]
     nx = mine.shape[0]
     core = lax.axis_index("core")
+    here = lax.axis_index("xa") * lax.axis_size("xb") + lax.axis_index("xb")
     width = shares.shape[2]
-
-    def run(halves):
-        left = jnp.concatenate([gathered[i, j] for i in range(ny) for j in range(nb)], axis=1)
-        for n in range(0, shares.shape[0], 2):
-            cols = slice(n * width, (n + 2) * width)
-            right = jnp.concatenate(
-                [
-                    half[x, i, j, :, cols]
-                    for i in range(ny)
-                    for j in range(nb)
-                    for x in range(nx)
-                    for half in halves
-                ],
-                axis=0,
-            )
-            both = jnp.dot(left, right, preferred_element_type=jnp.float32).astype(shares.dtype)
-            shares[n] = both[:, :width]
-            shares[n + 1] = both[:, width:]
-
-    @pl.when(core == 0)
-    def _():
-        run((mine, other))
-
-    @pl.when(core == 1)
-    def _():
-        run((other, mine))
+    moves = []
+    for d in range(nx):
+        x = lax.rem(here - d + nx, nx)
+        moves.append(pltpu.make_async_copy(mine.at[d], buffer.at[x, core], sems.at[2 * d]))
+        moves.append(
+            pltpu.make_async_copy(other.at[d], buffer.at[x, 1 - core], sems.at[2 * d + 1])
+        )
+    for move in moves:
+        move.start()
+    left = jnp.concatenate([gathered[i, j] for i in range(ny) for j in range(nb)], axis=1)
+    for move in moves:
+        move.wait()
+    for n in range(0, shares.shape[0], 2):
+        cols = slice(n * width, (n + 2) * width)
+        right = jnp.concatenate(
+            [
+                buffer[x, c, i, j, :, cols]
+                for i in range(ny)
+                for j in range(nb)
+                for x in range(nx)
+                for c in range(2)
+            ],
+            axis=0,
+        )
+        both = jnp.dot(left, right, preferred_element_type=jnp.float32).astype(shares.dtype)
+        shares[n] = both[:, :width]
+        shares[n + 1] = both[:, width:]
 
 
 def moved(value, axis, pairs):
@@ -214,13 +219,6 @@
 
 def near_vmem(value):
     return pltpu.with_memory_space_constraint(value, pltpu.VMEM)
-
-
-def everyone(value, axis):
-    count = lax.axis_size(axis)
-    return lax.all_to_all(
-        jnp.broadcast_to(value[None], (count,) + value.shape), axis, 0, 0, tiled=True
-    )
 
 
 def own_weights(out_weight):
@@ -242,12 +240,9 @@
     rows, chans = key_proj.shape
     modes = decay_rate.shape[0]
     na, nb = lax.axis_size("za"), lax.axis_size("zb")
-    ncore, nx, nw = (lax.axis_size(a) for a in ("core", X, "w"))
+    ncore, nw = lax.axis_size("core"), lax.axis_size("w")
     f32 = jnp.float32
     weights = own_weights(out_weight)
-    tails = jnp.stack([query_proj[rows - 2 :], key_proj[rows - 2 :], value_proj[rows - 2 :]], 0)
-    near = [(i, i + 1) for i in range(nw * nx * ncore - 1) if (i + 1) % (nx * ncore) > 0]
-    tails = moved(tails, CTX, near)
     featq, product, prefix, message = pl.pallas_call(
         first_pass,
         out_shape=(
@@ -256,56 +251,71 @@
             jax.ShapeDtypeStruct((modes, CHUNKS, chans), f32),
             pltpu.VMEM((modes + 16, chans), f32),
         ),
-        in_specs=[pl.BlockSpec(memory_space=pltpu.VMEM)] * 6,
+        in_specs=[pl.BlockSpec(memory_space=pltpu.VMEM)] * 5,
         out_specs=(pl.BlockSpec(memory_space=pltpu.VMEM),) * 4,
         scratch_shapes=[pltpu.VMEM((rows + 8, chans), f32), pltpu.VMEM((rows, chans), f32)],
         name="first_pass",
-    )(query_proj, key_proj, value_proj, near_vmem(tails), short_filter, decay_rate)
-
-    def join(value, axis, span):
-        count = lax.axis_size(axis)
-        rest = [
-            moved(value, axis, [(i, (i + d) % count) for i in range(count)])
-            for d in range(1, count)
-        ]
+    )(query_proj, key_proj, value_proj, short_filter, decay_rate)
+
+    def join(value, axis, lower, span):
+        other = moved(value, axis, [(0, 1), (1, 0)])
         return pl.pallas_call(
-            partial(joined, axis=axis, span=span),
+            partial(joined, axis=axis, lower=lower, span=span),
             out_shape=(
                 pltpu.VMEM((modes + 16, chans), f32),
                 pltpu.VMEM((modes, chans), f32),
+                pltpu.VMEM((8, chans), f32),
             ),
-            in_specs=[pl.BlockSpec(memory_space=pltpu.VMEM)] * (count + 1),
-            out_specs=(pl.BlockSpec(memory_space=pltpu.VMEM),) * 2,
-        )(decay_rate, near_vmem(value), *[near_vmem(r) for r in rest])
-
-    message, low = join(message, "core", rows)
-    message, mid = join(message, "xb", rows * ncore)
-    own, high = join(message, "xa", rows * ncore * lax.axis_size("xb"))
+            in_specs=[pl.BlockSpec(memory_space=pltpu.VMEM)] * 4,
+            out_specs=(pl.BlockSpec(memory_space=pltpu.VMEM),) * 3,
+        )(decay_rate, short_filter, near_vmem(value), near_vmem(other))
+
+    message, low, fix_low = join(message, "core", (), rows)
+    message, mid, fix_mid = join(message, "xb", ("core",), rows * ncore)
+    own, high, fix_high = join(message, "xa", ("xb", "core"), rows * ncore * lax.axis_size("xb"))
     back = {}
     back[1] = moved(own, "w", [(i, i + 1) for i in range(nw - 1)])
     back[3] = moved(own, "w", [(0, nw - 1)])
-    weights = everyone(weights, X)
+    nx = lax.axis_size(X)
+    pieces = [weights] + [
+        moved(weights, X, [(i, (i + d) % nx) for i in range(nx)]) for d in (2, 1, 3)
+    ]
+    pieces = [pieces[0], pieces[2], pieces[1], pieces[3]]
     held = jnp.where(lax.axis_index("w") == nw - 1, back[3], back[1])
     back[2] = moved(held, "w", [(nw - 2, nw - 1), (nw - 1, nw - 2)])
     gated = pl.pallas_call(
         second_pass,
         out_shape=jax.ShapeDtypeStruct((rows, chans), jnp.bfloat16),
         scratch_shapes=[pltpu.VMEM((rows, chans), f32), pltpu.VMEM((rows, chans), f32)],
-        in_specs=[pl.BlockSpec(memory_space=pltpu.VMEM)] * 14,
+        in_specs=[pl.BlockSpec(memory_space=pltpu.VMEM)] * 17,
         out_specs=pl.BlockSpec(memory_space=pltpu.VMEM),
         name="second_pass",
     )(
-        featq, product, prefix, *[near_vmem(v) for v in (low, mid, high, own)],
+        featq, product, prefix, *[near_vmem(v) for v in (low, mid, high, fix_low, fix_mid, fix_high, own)],
         *[near_vmem(back[d]) for d in (1, 2, 3)],
         short_filter, decay_rate, residue, skip_gain[None],
     )
-    other = moved(weights, "core", [(0, 1), (1, 0)])
     quarter = rows // nb
     mine = lax.all_to_all(gated.reshape(nb, quarter, chans), "zb", 0, 0, tiled=True)
-    gathered = everyone(mine, "y")
+    *pieces, mine = lax.optimization_barrier((*pieces, mine))
+    weights = jnp.stack(pieces, 0)
+    other = moved(weights, "core", [(0, 1), (1, 0)])
+    ny = lax.axis_size("y")
+    copies = near_vmem(jnp.broadcast_to(mine[None], (ny,) + mine.shape))
+    gathered = lax.all_to_all(copies, "y", 0, 0, tiled=True)
     shares = pl.pallas_call(
         project,
         out_shape=jax.ShapeDtypeStruct((na * nb, quarter, chans), jnp.bfloat16),
+        in_specs=[
+            pl.BlockSpec(memory_space=pltpu.VMEM),
+            pl.BlockSpec(memory_space=pl.ANY),
+            pl.BlockSpec(memory_space=pl.ANY),
+        ],
+        out_specs=pl.BlockSpec(memory_space=pltpu.VMEM),
+        scratch_shapes=[
+            pltpu.VMEM((nx, ncore) + weights.shape[1:], jnp.bfloat16),
+            pltpu.SemaphoreType.DMA((2 * nx,)),
+        ],
         name="project",
     )(gathered, weights, other)
     parts = lax.all_to_all(shares, ("za", "zb"), 0, 0, tiled=True)

time: 170 us -> 161 us (0.947)
  the two profiles are of different devices: /device:TPU:774 before, /device:TPU:768 now
where the time goes in v1:
time: 161 us; the launch traced here: 160 us
  blocking collectives  55.5 us (34%)
  starting transfers between devices  43.4 us (27%)
  waiting for transfers between devices  43.3 us (27%)
  Pallas kernels  14.5 us (9%)
  local copies, waits for them, and re-layouts  2.41 us (1%)
    ppermute x10, waiting for transfers between devices, moved(): return lax.ppermute(value, axis, pairs)  43.3 us
    all_to_all x1, blocking collectives, layer(): parts = lax.all_to_all(shares, ('za', 'zb'), 0, 0, tiled=True)  34.7 us
    ppermute x10, starting transfers between devices, moved(): return lax.ppermute(value, axis, pairs)  32.3 us
    all_to_all x1, blocking collectives, layer(): gathered = lax.all_to_all(copies, 'y', 0, 0, tiled=True)  20.8 us
    all_to_all x1, starting transfers between devices, own_weights(): got = lax.all_to_all(blocks, ('y', 'zb'), 0, 0, tiled=True)  5.94 us
    all_to_all x1, starting transfers between devices, layer(): lax.all_to_all(gated.reshape(nb, quarter, chans), 'zb', 0, 0, tiled=True)  5.09 us
    pallas_call x1, Pallas kernels, layer(): pl.pallas_call(project, out_shape=jax.ShapeDtypeStruct((na * nb, quarter,...  4.28 us
    pallas_call x1, Pallas kernels, layer(): pl.pallas_call(second_pass, out_shape=jax.ShapeDtypeStruct((rows, chans),...  4.18 us
  transfers between devices with their start and end apart: 12, of which 8 were waited for; matrix products, arithmetic and copies ran while one was open for 0% of the time, Pallas kernels for 6%

profile of v1, /device:TPU:768, one launch (start us, length us, event | category | flops | bytes accessed | tf_op | source)
XLA Modules:
  0.0 160.3 jit_solution(8356106567538178528)
XLA Ops:
  2.2 5.9 %all-to-all-start = ((bf16[16,16,1024]{2,1,0:T(8,128)(2,1)}), bf16[16,16,1024]{2,1,0:T(8,128)(2,1)S(1)}, u32[]{:S(2)}, u32[]{:S(2)}) async-start(bf16[16,16,1024]{2,1,0:T(8,128)(2,1)} %bitcast.1), calls=%async_computation | async-start | bytes 1048576 | tf_op jit(solution)/shard_map/all_to_all | solution.py:233
  8.2 3.8 %first_pass.1 = (f32[1024,128]{1,0:T(8,128)}, f32[1024,128]{1,0:T(8,128)}, f32[16,8,128]{2,1,0:T(8,128)}, f32[32,128]{1,0:T(8,128)S(1)}) custom-call(bf16[1024,128]{1,0:T(8,128)(2,1)} %q.1, bf16[1024,128]{1,0:T(8,128)(2,1)} %k.1, bf16[1024,128]{1,0:T(8,128)(2,1)} %v.1, bf16[3,3,128]{2,1,0:T(4,128)(2,1)} %taps.9, f32[16,128]{1,0:T(8,128)} %rates.9), custom_call_target="tpu_custom_call" | custom-call | tf_op jit(solution)/shard_map/first_pass/pallas_call | solution.py:246
  12.0 1.9 %collective-permute-start.3 = (f32[32,128]{1,0:T(8,128)S(1)}, f32[32,128]{1,0:T(8,128)S(1)}, u32[]{:S(2)}, u32[]{:S(2)}) collective-permute-start(f32[32,128]{1,0:T(8,128)S(1)} %get-tuple-element.26.own), channel_id=1, source_target_pairs={{0,1},{1,0},{2,3},{3,2},{4,5},{5,4},{6,7},{7,6},{8,9},{9,8},{10,11... | collective-permute-start | bytes 49160 | tf_op jit(solution)/shard_map/ppermute | solution.py:217
  15.8 3.4 %collective-permute-start.4 = (f32[32,128]{1,0:T(8,128)S(1)}, f32[32,128]{1,0:T(8,128)S(1)}, u32[]{:S(2)}, u32[]{:S(2)}) collective-permute-start(f32[32,128]{1,0:T(8,128)S(1)} %get-tuple-element.28.own), channel_id=1, source_target_pairs={{0,2},{2,0},{1,3},{3,1},{4,6},{6,4},{5,7},{7,5},{8,10},{10,8},{9,1... | collective-permute-start | bytes 49160 | tf_op jit(solution)/shard_map/ppermute | solution.py:217
  19.2 2.2 %collective-permute-done.4.other = f32[32,128]{1,0:T(8,128)S(1)} collective-permute-done((f32[32,128]{1,0:T(8,128)S(1)}, f32[32,128]{1,0:T(8,128)S(1)}, u32[]{:S(2)}, u32[]{:S(2)}) %collective-permute-start.4) | collective-permute-done | bytes 16416 | tf_op jit(solution)/shard_map/ppermute | solution.py:217
  22.1 4.9 %collective-permute-start.5 = (f32[32,128]{1,0:T(8,128)S(1)}, f32[32,128]{1,0:T(8,128)S(1)}, u32[]{:S(2)}, u32[]{:S(2)}) collective-permute-start(f32[32,128]{1,0:T(8,128)S(1)} %get-tuple-element.30.own), channel_id=1, source_target_pairs={{0,4},{4,0},{1,5},{5,1},{2,6},{6,2},{3,7},{7,3},{8,12},{12,8},{9,1... | collective-permute-start | bytes 49160 | tf_op jit(solution)/shard_map/ppermute | solution.py:217
  27.1 2.2 %collective-permute-done.5.other = f32[32,128]{1,0:T(8,128)S(1)} collective-permute-done((f32[32,128]{1,0:T(8,128)S(1)}, f32[32,128]{1,0:T(8,128)S(1)}, u32[]{:S(2)}, u32[]{:S(2)}) %collective-permute-start.5) | collective-permute-done | bytes 16416 | tf_op jit(solution)/shard_map/ppermute | solution.py:217
  30.0 1.3 collective-permute-start.7
  31.3 1.3 collective-permute-start.6
  32.6 11.9 %collective-permute-done.7.back3 = f32[32,128]{1,0:T(8,128)S(1)} collective-permute-done((f32[32,128]{1,0:T(8,128)S(1)}, f32[32,128]{1,0:T(8,128)S(1)}, u32[]{:S(2)}, u32[]{:S(2)}) %collective-permute-start.7) | collective-permute-done | bytes 16416 | tf_op jit(solution)/shard_map/ppermute | solution.py:217
  44.5 1.5 collective-permute-done.6.back1
  46.0 7.4 %collective-permute-start.8 = (f32[32,128]{1,0:T(8,128)S(1)}, f32[32,128]{1,0:T(8,128)S(1)}, u32[]{:S(2)}, u32[]{:S(2)}) collective-permute-start(f32[32,128]{1,0:T(8,128)S(1)} %broadcast_select_fusion), channel_id=1, source_target_pairs={{16,24},{24,16},{17,25},{25,17},{18,26},{26,18},{19,27},{27,19},{2... | collective-permute-start | bytes 49160 | tf_op jit(solution)/shard_map/ppermute | solution.py:217
  53.5 6.9 %collective-permute-done.8.back2 = f32[32,128]{1,0:T(8,128)S(1)} collective-permute-done((f32[32,128]{1,0:T(8,128)S(1)}, f32[32,128]{1,0:T(8,128)S(1)}, u32[]{:S(2)}, u32[]{:S(2)}) %collective-permute-start.8) | collective-permute-done | bytes 16416 | tf_op jit(solution)/shard_map/ppermute | solution.py:217
  60.4 4.2 %second_pass.1 = bf16[1024,128]{1,0:T(8,128)(2,1)} custom-call(f32[1024,128]{1,0:T(8,128)} %get-tuple-element.23.featq, f32[1024,128]{1,0:T(8,128)} %get-tuple-element.24.product, f32[16,8,128]{2,1,0:T(8,128)} %get-tuple-element.25.prefix, f32[16,128]{1,0:T(8,128)S(1)} %get-tuple-element.27.low, f32[16,128]{1,0:T(8,128)S(1)} %get-tuple-element.29.mid, ...), custom_call_target="tpu_custom_call" | custom-call | tf_op jit(solution)/shard_map/second_pass/pallas_call | solution.py:286
  64.6 5.1 %all-to-all-start.1 = ((bf16[4,256,128]{2,1,0:T(8,128)(2,1)}), bf16[4,256,128]{2,1,0:T(8,128)(2,1)S(1)}, u32[]{:S(2)}, u32[]{:S(2)}) async-start(bf16[4,256,128]{2,1,0:T(8,128)(2,1)} %bitcast.17), calls=%async_computation.1 | async-start | bytes 524288 | tf_op jit(solution)/shard_map/all_to_all | solution.py:299
  69.7 4.7 %collective-permute-start.2 = (bf16[4,4,16,1024]{3,2,1,0:T(8,128)(2,1)S(1)}, bf16[4,4,16,1024]{3,2,1,0:T(8,128)(2,1)S(1)}, u32[]{:S(2)}, u32[]{:S(2)}) collective-permute-start(bf16[4,4,16,1024]{3,2,1,0:T(8,128)(2,1)S(1)} %bitcast.13), channel_id=1, source_target_pairs={{0,6},{2,0},{4,2},{6,4},{1,7},{3,1},{5,3},{7,5},{8,14},{10,8},{12,... | collective-permute-start | bytes 1572872 | tf_op jit(solution)/shard_map/ppermute | solution.py:217
  74.3 2.7 %collective-permute-start.1 = (bf16[4,4,16,1024]{3,2,1,0:T(8,128)(2,1)S(1)}, bf16[4,4,16,1024]{3,2,1,0:T(8,128)(2,1)S(1)}, u32[]{:S(2)}, u32[]{:S(2)}) collective-permute-start(bf16[4,4,16,1024]{3,2,1,0:T(8,128)(2,1)S(1)} %bitcast.14), channel_id=1, source_target_pairs={{0,4},{2,6},{4,0},{6,2},{1,5},{3,7},{5,1},{7,3},{8,12},{10,14},{12... | collective-permute-start | bytes 1572872 | tf_op jit(solution)/shard_map/ppermute | solution.py:217
  77.0 2.8 %collective-permute-start = (bf16[4,4,16,1024]{3,2,1,0:T(8,128)(2,1)S(1)}, bf16[4,4,16,1024]{3,2,1,0:T(8,128)(2,1)S(1)}, u32[]{:S(2)}, u32[]{:S(2)}) collective-permute-start(bf16[4,4,16,1024]{3,2,1,0:T(8,128)(2,1)S(1)} %bitcast.15), channel_id=1, source_target_pairs={{0,2},{2,4},{4,6},{6,0},{1,3},{3,5},{5,7},{7,1},{8,10},{10,12},{12... | collective-permute-start | bytes 1572872 | tf_op jit(solution)/shard_map/ppermute | solution.py:217
  79.8 11.8 %collective-permute-done.2 = bf16[4,4,16,1024]{3,2,1,0:T(8,128)(2,1)S(1)} collective-permute-done((bf16[4,4,16,1024]{3,2,1,0:T(8,128)(2,1)S(1)}, bf16[4,4,16,1024]{3,2,1,0:T(8,128)(2,1)S(1)}, u32[]{:S(2)}, u32[]{:S(2)}) %collective-permute-start.2) | collective-permute-done | bytes 524320 | tf_op jit(solution)/shard_map/ppermute | solution.py:217
  91.7 5.6 %collective-permute-done = bf16[4,4,16,1024]{3,2,1,0:T(8,128)(2,1)S(1)} collective-permute-done((bf16[4,4,16,1024]{3,2,1,0:T(8,128)(2,1)S(1)}, bf16[4,4,16,1024]{3,2,1,0:T(8,128)(2,1)S(1)}, u32[]{:S(2)}, u32[]{:S(2)}) %collective-permute-start) | collective-permute-done | bytes 524320 | tf_op jit(solution)/shard_map/ppermute | solution.py:217
  97.6 1.9 %collective-permute-start.9 = (bf16[4,4,4,16,1024]{4,3,2,1,0:T(8,128)(2,1)S(1)}, bf16[4,4,4,16,1024]{4,3,2,1,0:T(8,128)(2,1)}, u32[]{:S(2)}, u32[]{:S(2)}) collective-permute-start(bf16[4,4,4,16,1024]{4,3,2,1,0:T(8,128)(2,1)S(1)} %pad_maximum_fusion.mine), channel_id=1, source_target_pairs={{0,1},{1,0},{2,3},{3,2},{4,5},{5,4},{6,7},{7,6},{8,9},{9,8},{10,11... | collective-permute-start | bytes 6291464 | tf_op jit(solution)/shard_map/ppermute | solution.py:217
  99.7 20.8 %all_to_all.20.gathered = bf16[4,4,256,128]{3,2,1,0:T(8,128)(2,1)S(1)} all-to-all(bf16[4,4,256,128]{3,2,1,0:T(8,128)(2,1)S(1)} %broadcast_in_dim.8), channel_id=1, replica_groups=mesh['y'=4,'za'=2,'zb'=4,'w'=4,'xa'=2,'xb'=2,'core'=2] {'y'}, dimensions={0} | all-to-all | bytes 2097152 | tf_op jit(solution)/shard_map/all_to_all | solution.py:305
  120.6 4.3 %project.1 = bf16[8,256,128]{2,1,0:T(8,128)(2,1)} custom-call(bf16[4,4,256,128]{3,2,1,0:T(8,128)(2,1)S(1)} %all_to_all.20.gathered, bf16[4,4,4,16,1024]{4,3,2,1,0:T(8,128)(2,1)} %copy-done.1, bf16[4,4,4,16,1024]{4,3,2,1,0:T(8,128)(2,1)} %collective-permute-done.9.other), custom_call_target="tpu_custom_call" | custom-call | tf_op jit(solution)/shard_map/project/pallas_call | solution.py:306
  124.8 34.7 %all_to_all.21 = bf16[8,256,128]{2,1,0:T(8,128)(2,1)S(1)} all-to-all(bf16[8,256,128]{2,1,0:T(8,128)(2,1)} %project.1), channel_id=1, replica_groups=mesh['y'=4,'za'=2,'zb'=4,'w'=4,'xa'=2,'xb'=2,'core'=2] {'za','zb'}, dimensions={0} | all-to-all | bytes 1048576 | tf_op jit(solution)/shard_map/all_to_all | solution.py:321
  (20 shorter events, 6.8 us)
Async XLA Ops:
  0.0 1.2 copy-start
  2.2 62.3 %all-to-all-start = ((bf16[16,16,1024]{2,1,0:T(8,128)(2,1)}), bf16[16,16,1024]{2,1,0:T(8,128)(2,1)S(1)}, u32[]{:S(2)}, u32[]{:S(2)}) async-start(bf16[16,16,1024]{2,1,0:T(8,128)(2,1)} %bitcast.1), calls=%async_computation | async-start | bytes 1048576 | tf_op jit(solution)/shard_map/all_to_all | solution.py:233
  12.0 3.1 %collective-permute-start.3 = (f32[32,128]{1,0:T(8,128)S(1)}, f32[32,128]{1,0:T(8,128)S(1)}, u32[]{:S(2)}, u32[]{:S(2)}) collective-permute-start(f32[32,128]{1,0:T(8,128)S(1)} %get-tuple-element.26.own), channel_id=1, source_target_pairs={{0,1},{1,0},{2,3},{3,2},{4,5},{5,4},{6,7},{7,6},{8,9},{9,8},{10,11... | collective-permute-start | bytes 49160 | tf_op jit(solution)/shard_map/ppermute | solution.py:217
  15.8 5.6 %collective-permute-start.4 = (f32[32,128]{1,0:T(8,128)S(1)}, f32[32,128]{1,0:T(8,128)S(1)}, u32[]{:S(2)}, u32[]{:S(2)}) collective-permute-start(f32[32,128]{1,0:T(8,128)S(1)} %get-tuple-element.28.own), channel_id=1, source_target_pairs={{0,2},{2,0},{1,3},{3,1},{4,6},{6,4},{5,7},{7,5},{8,10},{10,8},{9,1... | collective-permute-start | bytes 49160 | tf_op jit(solution)/shard_map/ppermute | solution.py:217
  22.1 7.1 %collective-permute-start.5 = (f32[32,128]{1,0:T(8,128)S(1)}, f32[32,128]{1,0:T(8,128)S(1)}, u32[]{:S(2)}, u32[]{:S(2)}) collective-permute-start(f32[32,128]{1,0:T(8,128)S(1)} %get-tuple-element.30.own), channel_id=1, source_target_pairs={{0,4},{4,0},{1,5},{5,1},{2,6},{6,2},{3,7},{7,3},{8,12},{12,8},{9,1... | collective-permute-start | bytes 49160 | tf_op jit(solution)/shard_map/ppermute | solution.py:217
  30.0 14.5 %collective-permute-start.7 = (f32[32,128]{1,0:T(8,128)S(1)}, f32[32,128]{1,0:T(8,128)S(1)}, u32[]{:S(2)}, u32[]{:S(2)}) collective-permute-start(f32[32,128]{1,0:T(8,128)S(1)} %get-tuple-element.35.own), channel_id=1, source_target_pairs={{0,24},{1,25},{2,26},{3,27},{4,28},{5,29},{6,30},{7,31},{32,56},{3... | collective-permute-start | bytes 49160 | tf_op jit(solution)/shard_map/ppermute | solution.py:217
  31.3 14.7 %collective-permute-start.6 = (f32[32,128]{1,0:T(8,128)S(1)}, f32[32,128]{1,0:T(8,128)S(1)}, u32[]{:S(2)}, u32[]{:S(2)}) collective-permute-start(f32[32,128]{1,0:T(8,128)S(1)} %get-tuple-element.35.own), channel_id=1, source_target_pairs={{0,8},{8,16},{16,24},{1,9},{9,17},{17,25},{2,10},{10,18},{18,26},{... | collective-permute-start | bytes 49160 | tf_op jit(solution)/shard_map/ppermute | solution.py:217
  46.0 14.3 %collective-permute-start.8 = (f32[32,128]{1,0:T(8,128)S(1)}, f32[32,128]{1,0:T(8,128)S(1)}, u32[]{:S(2)}, u32[]{:S(2)}) collective-permute-start(f32[32,128]{1,0:T(8,128)S(1)} %broadcast_select_fusion), channel_id=1, source_target_pairs={{16,24},{24,16},{17,25},{25,17},{18,26},{26,18},{19,27},{27,19},{2... | collective-permute-start | bytes 49160 | tf_op jit(solution)/shard_map/ppermute | solution.py:217
  64.6 15.3 %all-to-all-start.1 = ((bf16[4,256,128]{2,1,0:T(8,128)(2,1)}), bf16[4,256,128]{2,1,0:T(8,128)(2,1)S(1)}, u32[]{:S(2)}, u32[]{:S(2)}) async-start(bf16[4,256,128]{2,1,0:T(8,128)(2,1)} %bitcast.17), calls=%async_computation.1 | async-start | bytes 524288 | tf_op jit(solution)/shard_map/all_to_all | solution.py:299
  69.7 22.0 %collective-permute-start.2 = (bf16[4,4,16,1024]{3,2,1,0:T(8,128)(2,1)S(1)}, bf16[4,4,16,1024]{3,2,1,0:T(8,128)(2,1)S(1)}, u32[]{:S(2)}, u32[]{:S(2)}) collective-permute-start(bf16[4,4,16,1024]{3,2,1,0:T(8,128)(2,1)S(1)} %bitcast.13), channel_id=1, source_target_pairs={{0,6},{2,0},{4,2},{6,4},{1,7},{3,1},{5,3},{7,5},{8,14},{10,8},{12,... | collective-permute-start | bytes 1572872 | tf_op jit(solution)/shard_map/ppermute | solution.py:217
  74.3 17.4 %collective-permute-start.1 = (bf16[4,4,16,1024]{3,2,1,0:T(8,128)(2,1)S(1)}, bf16[4,4,16,1024]{3,2,1,0:T(8,128)(2,1)S(1)}, u32[]{:S(2)}, u32[]{:S(2)}) collective-permute-start(bf16[4,4,16,1024]{3,2,1,0:T(8,128)(2,1)S(1)} %bitcast.14), channel_id=1, source_target_pairs={{0,4},{2,6},{4,0},{6,2},{1,5},{3,7},{5,1},{7,3},{8,12},{10,14},{12... | collective-permute-start | bytes 1572872 | tf_op jit(solution)/shard_map/ppermute | solution.py:217
  77.0 20.3 %collective-permute-start = (bf16[4,4,16,1024]{3,2,1,0:T(8,128)(2,1)S(1)}, bf16[4,4,16,1024]{3,2,1,0:T(8,128)(2,1)S(1)}, u32[]{:S(2)}, u32[]{:S(2)}) collective-permute-start(bf16[4,4,16,1024]{3,2,1,0:T(8,128)(2,1)S(1)} %bitcast.15), channel_id=1, source_target_pairs={{0,2},{2,4},{4,6},{6,0},{1,3},{3,5},{5,7},{7,1},{8,10},{10,12},{12... | collective-permute-start | bytes 1572872 | tf_op jit(solution)/shard_map/ppermute | solution.py:217
  97.6 1.9 %copy-start.1 = (bf16[4,4,4,16,1024]{4,3,2,1,0:T(8,128)(2,1)}, bf16[4,4,4,16,1024]{4,3,2,1,0:T(8,128)(2,1)S(1)}, u32[]{:S(2)}) copy-start(bf16[4,4,4,16,1024]{4,3,2,1,0:T(8,128)(2,1)S(1)} %pad_maximum_fusion.mine) | copy-start | bytes 6291460
  97.6 23.0 %collective-permute-start.9 = (bf16[4,4,4,16,1024]{4,3,2,1,0:T(8,128)(2,1)S(1)}, bf16[4,4,4,16,1024]{4,3,2,1,0:T(8,128)(2,1)}, u32[]{:S(2)}, u32[]{:S(2)}) collective-permute-start(bf16[4,4,4,16,1024]{4,3,2,1,0:T(8,128)(2,1)S(1)} %pad_maximum_fusion.mine), channel_id=1, source_target_pairs={{0,1},{1,0},{2,3},{3,2},{4,5},{5,4},{6,7},{7,6},{8,9},{9,8},{10,11... | collective-permute-start | bytes 6291464 | tf_op jit(solution)/shard_map/ppermute | solution.py:217

commit v2 on v1

--- a/solution.py
+++ b/solution.py
@@ -178,39 +178,37 @@
     gated[0:16, :] = (query * long_out[0:16, :]).astype(jnp.bfloat16)
 
 
-def project(gathered, mine, other, shares, buffer, sems):
+def project(gathered, mine, other, shares):
     ny, nb = gathered.shape[:2]
     nx = mine.shape[0]
     core = lax.axis_index("core")
-    here = lax.axis_index("xa") * lax.axis_size("xb") + lax.axis_index("xb")
     width = shares.shape[2]
-    moves = []
-    for d in range(nx):
-        x = lax.rem(here - d + nx, nx)
-        moves.append(pltpu.make_async_copy(mine.at[d], buffer.at[x, core], sems.at[2 * d]))
-        moves.append(
-            pltpu.make_async_copy(other.at[d], buffer.at[x, 1 - core], sems.at[2 * d + 1])
-        )
-    for move in moves:
-        move.start()
-    left = jnp.concatenate([gathered[i, j] for i in range(ny) for j in range(nb)], axis=1)
-    for move in moves:
-        move.wait()
-    for n in range(0, shares.shape[0], 2):
-        cols = slice(n * width, (n + 2) * width)
-        right = jnp.concatenate(
-            [
-                buffer[x, c, i, j, :, cols]
-                for i in range(ny)
-                for j in range(nb)
-                for x in range(nx)
-                for c in range(2)
-            ],
-            axis=0,
-        )
-        both = jnp.dot(left, right, preferred_element_type=jnp.float32).astype(shares.dtype)
-        shares[n] = both[:, :width]
-        shares[n + 1] = both[:, width:]
+
+    def run(halves):
+        left = jnp.concatenate([gathered[i, j] for i in range(ny) for j in range(nb)], axis=1)
+        for n in range(0, shares.shape[0], 2):
+            cols = slice(n * width, (n + 2) * width)
+            right = jnp.concatenate(
+                [
+                    half[x, i, j, :, cols]
+                    for i in range(ny)
+                    for j in range(nb)
+                    for x in range(nx)
+                    for half in halves
+                ],
+                axis=0,
+            )
+            both = jnp.dot(left, right, preferred_element_type=jnp.float32).astype(shares.dtype)
+            shares[n] = both[:, :width]
+            shares[n + 1] = both[:, width:]
+
+    @pl.when(core == 0)
+    def _():
+        run((mine, other))
+
+    @pl.when(core == 1)
+    def _():
+        run((other, mine))
 
 
 def moved(value, axis, pairs):
@@ -219,6 +217,13 @@
 
 def near_vmem(value):
     return pltpu.with_memory_space_constraint(value, pltpu.VMEM)
+
+
+def everyone(value, axis):
+    count = lax.axis_size(axis)
+    return lax.all_to_all(
+        jnp.broadcast_to(value[None], (count,) + value.shape), axis, 0, 0, tiled=True
+    )
 
 
 def own_weights(out_weight):
@@ -276,11 +281,7 @@
     back = {}
     back[1] = moved(own, "w", [(i, i + 1) for i in range(nw - 1)])
     back[3] = moved(own, "w", [(0, nw - 1)])
-    nx = lax.axis_size(X)
-    pieces = [weights] + [
-        moved(weights, X, [(i, (i + d) % nx) for i in range(nx)]) for d in (2, 1, 3)
-    ]
-    pieces = [pieces[0], pieces[2], pieces[1], pieces[3]]
+    weights = everyone(weights, X)
     held = jnp.where(lax.axis_index("w") == nw - 1, back[3], back[1])
     back[2] = moved(held, "w", [(nw - 2, nw - 1), (nw - 1, nw - 2)])
     gated = pl.pallas_call(
@@ -295,27 +296,15 @@
         *[near_vmem(back[d]) for d in (1, 2, 3)],
         short_filter, decay_rate, residue, skip_gain[None],
     )
+    other = moved(weights, "core", [(0, 1), (1, 0)])
     quarter = rows // nb
     mine = lax.all_to_all(gated.reshape(nb, quarter, chans), "zb", 0, 0, tiled=True)
-    *pieces, mine = lax.optimization_barrier((*pieces, mine))
-    weights = jnp.stack(pieces, 0)
-    other = moved(weights, "core", [(0, 1), (1, 0)])
     ny = lax.axis_size("y")
     copies = near_vmem(jnp.broadcast_to(mine[None], (ny,) + mine.shape))
     gathered = lax.all_to_all(copies, "y", 0, 0, tiled=True)
     shares = pl.pallas_call(
         project,
         out_shape=jax.ShapeDtypeStruct((na * nb, quarter, chans), jnp.bfloat16),
-        in_specs=[
-            pl.BlockSpec(memory_space=pltpu.VMEM),
-            pl.BlockSpec(memory_space=pl.ANY),
-            pl.BlockSpec(memory_space=pl.ANY),
-        ],
-        out_specs=pl.BlockSpec(memory_space=pltpu.VMEM),
-        scratch_shapes=[
-            pltpu.VMEM((nx, ncore) + weights.shape[1:], jnp.bfloat16),
-            pltpu.SemaphoreType.DMA((2 * nx,)),
-        ],
         name="project",
     )(gathered, weights, other)
     parts = lax.all_to_all(shares, ("za", "zb"), 0, 0, tiled=True)

time: 161 us -> 159 us (0.988)
  starting transfers between devices: 43.4 us -> 30.5 us
  blocking collectives: 55.5 us -> 68.2 us
  waiting for transfers between devices: 43.3 us -> 41 us
    all_to_all x0 -> x1, blocking collectives: none -> 22.2 us  [own_weights(): got = lax.all_to_all(blocks, ('y', 'zb'), 0, 0, tiled=True)]
    ppermute x10 -> x7, starting transfers between devices: 32.3 us -> 22.7 us  [moved(): return lax.ppermute(value, axis, pairs)]
    ppermute x10 -> x7, waiting for transfers between devices: 43.3 us -> 36.2 us  [moved(): return lax.ppermute(value, axis, pairs)]
    all_to_all x1, blocking collectives: 20.8 us -> 13.7 us  [layer(): gathered = lax.all_to_all(copies, 'y', 0, 0, tiled=True)]
    all_to_all x1, waiting for transfers between devices: 0.01 us -> 4.81 us  [layer(): lax.all_to_all(gated.reshape(nb, quarter, chans), 'zb', 0, 0, tiled=True)]
    all_to_all x1, blocking collectives: 34.7 us -> 32.3 us  [layer(): parts = lax.all_to_all(shares, ('za', 'zb'), 0, 0, tiled=True)]
    all_to_all x1, starting transfers between devices: 5.09 us -> 3.41 us  [layer(): lax.all_to_all(gated.reshape(nb, quarter, chans), 'zb', 0, 0, tiled=True)]
  transfers between devices with their start and end apart: 12 -> 9, of which waited for: 8 -> 7; matrix products, arithmetic and copies ran while one was open for 0% -> 0% of each run, Pallas kernels for 6% -> 6%
where the time goes in v2:
time: 159 us; the launch traced here: 158 us
  blocking collectives  68.2 us (43%)
  waiting for transfers between devices  41 us (26%)
  starting transfers between devices  30.5 us (19%)
  Pallas kernels  14.4 us (9%)
  local copies, waits for them, and re-layouts  3.2 us (2%)
    ppermute x7, waiting for transfers between devices, moved(): return lax.ppermute(value, axis, pairs)  36.2 us
    all_to_all x1, blocking collectives, layer(): parts = lax.all_to_all(shares, ('za', 'zb'), 0, 0, tiled=True)  32.3 us
    ppermute x7, starting transfers between devices, moved(): return lax.ppermute(value, axis, pairs)  22.7 us
    all_to_all x1, blocking collectives, own_weights(): got = lax.all_to_all(blocks, ('y', 'zb'), 0, 0, tiled=True)  22.2 us
    all_to_all x1, blocking collectives, layer(): gathered = lax.all_to_all(copies, 'y', 0, 0, tiled=True)  13.7 us
    all_to_all x1, waiting for transfers between devices, layer(): lax.all_to_all(gated.reshape(nb, quarter, chans), 'zb', 0, 0, tiled=True)  4.81 us
    all_to_all x1, starting transfers between devices, everyone(): lax.all_to_all(jnp.broadcast_to(value[None], (count,) + value.shape), axi...  4.45 us
    pallas_call x1, Pallas kernels, layer(): pl.pallas_call(project, out_shape=jax.ShapeDtypeStruct((na * nb, quarter,...  4.26 us
  transfers between devices with their start and end apart: 9, of which 7 were waited for; matrix products, arithmetic and copies ran while one was open for 0% of the time, Pallas kernels for 6%

profile of v2, /device:TPU:768, one launch (start us, length us, event | category | flops | bytes accessed | tf_op | source)
XLA Modules:
  0.0 158.3 jit_solution(8863340175480045365)
XLA Ops:
  0.0 1.2 copy-done
  1.4 22.2 %all_to_all.25 = bf16[16,16,1024]{2,1,0:T(8,128)(2,1)S(1)} all-to-all(bf16[16,16,1024]{2,1,0:T(8,128)(2,1)S(1)} %bitcast.9), channel_id=1, replica_groups=mesh['y'=4,'za'=2,'zb'=4,'w'=4,'xa'=2,'xb'=2,'core'=2] {'y','zb'}, dimensions={0} | all-to-all | bytes 1048576 | tf_op jit(solution)/shard_map/all_to_all | solution.py:238
  23.7 1.6 %broadcast_in_dim.26 = bf16[4,4,4,16,1024]{4,3,2,1,0:T(8,128)(2,1)} broadcast(bf16[4,4,16,1024]{3,2,1,0:T(8,128)(2,1)S(1)} %bitcast.8), dimensions={1,2,3,4} | broadcast | bytes 2621440 | tf_op jit(solution)/shard_map/broadcast_in_dim | solution.py:225
  25.3 4.4 %all-to-all-start.3 = ((bf16[4,4,4,16,1024]{4,3,2,1,0:T(8,128)(2,1)}), bf16[4,4,4,16,1024]{4,3,2,1,0:T(8,128)(2,1)}, u32[]{:S(2)}, u32[]{:S(2)}) async-start(bf16[4,4,4,16,1024]{4,3,2,1,0:T(8,128)(2,1)} %broadcast_in_dim.26), calls=%async_computation.3 | async-start | bytes 4194304 | tf_op jit(solution)/shard_map/all_to_all | solution.py:224
  29.7 3.8 %first_pass.1 = (f32[1024,128]{1,0:T(8,128)}, f32[1024,128]{1,0:T(8,128)}, f32[16,8,128]{2,1,0:T(8,128)}, f32[32,128]{1,0:T(8,128)S(1)}) custom-call(bf16[1024,128]{1,0:T(8,128)(2,1)} %q.1, bf16[1024,128]{1,0:T(8,128)(2,1)} %k.1, bf16[1024,128]{1,0:T(8,128)(2,1)} %v.1, bf16[3,3,128]{2,1,0:T(4,128)(2,1)} %taps.9, f32[16,128]{1,0:T(8,128)} %rates.9), custom_call_target="tpu_custom_call" | custom-call | tf_op jit(solution)/shard_map/first_pass/pallas_call | solution.py:251
  33.5 1.9 %collective-permute-start = (f32[32,128]{1,0:T(8,128)S(1)}, f32[32,128]{1,0:T(8,128)S(1)}, u32[]{:S(2)}, u32[]{:S(2)}) collective-permute-start(f32[32,128]{1,0:T(8,128)S(1)} %get-tuple-element.21.own), channel_id=1, source_target_pairs={{0,1},{1,0},{2,3},{3,2},{4,5},{5,4},{6,7},{7,6},{8,9},{9,8},{10,11... | collective-permute-start | bytes 49160 | tf_op jit(solution)/shard_map/ppermute | solution.py:215
  35.4 1.1 collective-permute-done.other
  37.3 3.9 %collective-permute-start.1 = (f32[32,128]{1,0:T(8,128)S(1)}, f32[32,128]{1,0:T(8,128)S(1)}, u32[]{:S(2)}, u32[]{:S(2)}) collective-permute-start(f32[32,128]{1,0:T(8,128)S(1)} %get-tuple-element.23.own), channel_id=1, source_target_pairs={{0,2},{2,0},{1,3},{3,1},{4,6},{6,4},{5,7},{7,5},{8,10},{10,8},{9,1... | collective-permute-start | bytes 49160 | tf_op jit(solution)/shard_map/ppermute | solution.py:215
  41.2 12.9 %collective-permute-done.1.other = f32[32,128]{1,0:T(8,128)S(1)} collective-permute-done((f32[32,128]{1,0:T(8,128)S(1)}, f32[32,128]{1,0:T(8,128)S(1)}, u32[]{:S(2)}, u32[]{:S(2)}) %collective-permute-start.1) | collective-permute-done | bytes 16416 | tf_op jit(solution)/shard_map/ppermute | solution.py:215
  54.9 4.6 %collective-permute-start.2 = (f32[32,128]{1,0:T(8,128)S(1)}, f32[32,128]{1,0:T(8,128)S(1)}, u32[]{:S(2)}, u32[]{:S(2)}) collective-permute-start(f32[32,128]{1,0:T(8,128)S(1)} %get-tuple-element.25.own), channel_id=1, source_target_pairs={{0,4},{4,0},{1,5},{5,1},{2,6},{6,2},{3,7},{7,3},{8,12},{12,8},{9,1... | collective-permute-start | bytes 49160 | tf_op jit(solution)/shard_map/ppermute | solution.py:215
  59.4 2.5 %collective-permute-done.2.other = f32[32,128]{1,0:T(8,128)S(1)} collective-permute-done((f32[32,128]{1,0:T(8,128)S(1)}, f32[32,128]{1,0:T(8,128)S(1)}, u32[]{:S(2)}, u32[]{:S(2)}) %collective-permute-start.2) | collective-permute-done | bytes 16416 | tf_op jit(solution)/shard_map/ppermute | solution.py:215
  62.7 1.3 collective-permute-start.4
  64.0 1.3 collective-permute-start.3
  65.3 11.7 %collective-permute-done.4.back3 = f32[32,128]{1,0:T(8,128)S(1)} collective-permute-done((f32[32,128]{1,0:T(8,128)S(1)}, f32[32,128]{1,0:T(8,128)S(1)}, u32[]{:S(2)}, u32[]{:S(2)}) %collective-permute-start.4) | collective-permute-done | bytes 16416 | tf_op jit(solution)/shard_map/ppermute | solution.py:215
  77.1 1.3 collective-permute-done.3.back1
  78.4 7.8 %collective-permute-start.5 = (f32[32,128]{1,0:T(8,128)S(1)}, f32[32,128]{1,0:T(8,128)S(1)}, u32[]{:S(2)}, u32[]{:S(2)}) collective-permute-start(f32[32,128]{1,0:T(8,128)S(1)} %broadcast_select_fusion), channel_id=1, source_target_pairs={{16,24},{24,16},{17,25},{25,17},{18,26},{26,18},{19,27},{27,19},{2... | collective-permute-start | bytes 49160 | tf_op jit(solution)/shard_map/ppermute | solution.py:215
  86.2 6.5 %collective-permute-done.5.back2 = f32[32,128]{1,0:T(8,128)S(1)} collective-permute-done((f32[32,128]{1,0:T(8,128)S(1)}, f32[32,128]{1,0:T(8,128)S(1)}, u32[]{:S(2)}, u32[]{:S(2)}) %collective-permute-start.5) | collective-permute-done | bytes 16416 | tf_op jit(solution)/shard_map/ppermute | solution.py:215
  92.7 4.2 %second_pass.1 = bf16[1024,128]{1,0:T(8,128)(2,1)} custom-call(f32[1024,128]{1,0:T(8,128)} %get-tuple-element.18.featq, f32[1024,128]{1,0:T(8,128)} %get-tuple-element.19.product, f32[16,8,128]{2,1,0:T(8,128)} %get-tuple-element.20.prefix, f32[16,128]{1,0:T(8,128)S(1)} %get-tuple-element.22.low, f32[16,128]{1,0:T(8,128)S(1)} %get-tuple-element.24.mid, ...), custom_call_target="tpu_custom_call" | custom-call | tf_op jit(solution)/shard_map/second_pass/pallas_call | solution.py:287
  96.9 3.4 %all-to-all-start = ((bf16[4,256,128]{2,1,0:T(8,128)(2,1)}), bf16[4,256,128]{2,1,0:T(8,128)(2,1)S(1)}, u32[]{:S(2)}, u32[]{:S(2)}) async-start(bf16[4,256,128]{2,1,0:T(8,128)(2,1)} %bitcast.11), calls=%async_computation | async-start | bytes 524288 | tf_op jit(solution)/shard_map/all_to_all | solution.py:301
  100.3 1.9 %collective-permute-start.6 = (bf16[4,4,4,16,1024]{4,3,2,1,0:T(8,128)(2,1)}, bf16[4,4,4,16,1024]{4,3,2,1,0:T(8,128)(2,1)}, u32[]{:S(2)}, u32[]{:S(2)}) collective-permute-start(bf16[4,4,4,16,1024]{4,3,2,1,0:T(8,128)(2,1)} %all-to-all-done.3.mine), channel_id=1, source_target_pairs={{0,1},{1,0},{2,3},{3,2},{4,5},{5,4},{6,7},{7,6},{8,9},{9,8},{10,11... | collective-permute-start | bytes 6291464 | tf_op jit(solution)/shard_map/ppermute | solution.py:215
  102.3 4.8 %all-to-all-done = bf16[4,256,128]{2,1,0:T(8,128)(2,1)S(1)} async-done(((bf16[4,256,128]{2,1,0:T(8,128)(2,1)}), bf16[4,256,128]{2,1,0:T(8,128)(2,1)S(1)}, u32[]{:S(2)}, u32[]{:S(2)}) %all-to-all-start) | async-done | bytes 262176 | tf_op jit(solution)/shard_map/all_to_all | solution.py:301
  107.3 13.7 %all_to_all.26.gathered = bf16[4,4,256,128]{3,2,1,0:T(8,128)(2,1)S(1)} all-to-all(bf16[4,4,256,128]{3,2,1,0:T(8,128)(2,1)S(1)} %broadcast_in_dim.11), channel_id=1, replica_groups=mesh['y'=4,'za'=2,'zb'=4,'w'=4,'xa'=2,'xb'=2,'core'=2] {'y'}, dimensions={0} | all-to-all | bytes 2097152 | tf_op jit(solution)/shard_map/all_to_all | solution.py:304
  120.9 4.3 %project.1 = bf16[8,256,128]{2,1,0:T(8,128)(2,1)} custom-call(bf16[4,4,256,128]{3,2,1,0:T(8,128)(2,1)S(1)} %all_to_all.26.gathered, bf16[4,4,4,16,1024]{4,3,2,1,0:T(8,128)(2,1)} %all-to-all-done.3.mine, bf16[4,4,4,16,1024]{4,3,2,1,0:T(8,128)(2,1)} %collective-permute-done.6.other), custom_call_target="tpu_custom_call" | custom-call | tf_op jit(solution)/shard_map/project/pallas_call | solution.py:305
  125.2 32.3 %all_to_all.27 = bf16[8,256,128]{2,1,0:T(8,128)(2,1)S(1)} all-to-all(bf16[8,256,128]{2,1,0:T(8,128)(2,1)} %project.1), channel_id=1, replica_groups=mesh['y'=4,'za'=2,'zb'=4,'w'=4,'xa'=2,'xb'=2,'core'=2] {'za','zb'}, dimensions={0} | all-to-all | bytes 1048576 | tf_op jit(solution)/shard_map/all_to_all | solution.py:310
  (13 shorter events, 3.4 us)
Async XLA Ops:
  0.0 1.2 copy-start
  25.3 71.6 %all-to-all-start.3 = ((bf16[4,4,4,16,1024]{4,3,2,1,0:T(8,128)(2,1)}), bf16[4,4,4,16,1024]{4,3,2,1,0:T(8,128)(2,1)}, u32[]{:S(2)}, u32[]{:S(2)}) async-start(bf16[4,4,4,16,1024]{4,3,2,1,0:T(8,128)(2,1)} %broadcast_in_dim.26), calls=%async_computation.3 | async-start | bytes 4194304 | tf_op jit(solution)/shard_map/all_to_all | solution.py:224
  33.5 3.1 %collective-permute-start = (f32[32,128]{1,0:T(8,128)S(1)}, f32[32,128]{1,0:T(8,128)S(1)}, u32[]{:S(2)}, u32[]{:S(2)}) collective-permute-start(f32[32,128]{1,0:T(8,128)S(1)} %get-tuple-element.21.own), channel_id=1, source_target_pairs={{0,1},{1,0},{2,3},{3,2},{4,5},{5,4},{6,7},{7,6},{8,9},{9,8},{10,11... | collective-permute-start | bytes 49160 | tf_op jit(solution)/shard_map/ppermute | solution.py:215
  37.3 16.8 %collective-permute-start.1 = (f32[32,128]{1,0:T(8,128)S(1)}, f32[32,128]{1,0:T(8,128)S(1)}, u32[]{:S(2)}, u32[]{:S(2)}) collective-permute-start(f32[32,128]{1,0:T(8,128)S(1)} %get-tuple-element.23.own), channel_id=1, source_target_pairs={{0,2},{2,0},{1,3},{3,1},{4,6},{6,4},{5,7},{7,5},{8,10},{10,8},{9,1... | collective-permute-start | bytes 49160 | tf_op jit(solution)/shard_map/ppermute | solution.py:215
  54.9 7.1 %collective-permute-start.2 = (f32[32,128]{1,0:T(8,128)S(1)}, f32[32,128]{1,0:T(8,128)S(1)}, u32[]{:S(2)}, u32[]{:S(2)}) collective-permute-start(f32[32,128]{1,0:T(8,128)S(1)} %get-tuple-element.25.own), channel_id=1, source_target_pairs={{0,4},{4,0},{1,5},{5,1},{2,6},{6,2},{3,7},{7,3},{8,12},{12,8},{9,1... | collective-permute-start | bytes 49160 | tf_op jit(solution)/shard_map/ppermute | solution.py:215
  62.7 14.3 %collective-permute-start.4 = (f32[32,128]{1,0:T(8,128)S(1)}, f32[32,128]{1,0:T(8,128)S(1)}, u32[]{:S(2)}, u32[]{:S(2)}) collective-permute-start(f32[32,128]{1,0:T(8,128)S(1)} %get-tuple-element.30.own), channel_id=1, source_target_pairs={{0,24},{1,25},{2,26},{3,27},{4,28},{5,29},{6,30},{7,31},{32,56},{3... | collective-permute-start | bytes 49160 | tf_op jit(solution)/shard_map/ppermute | solution.py:215
  64.0 14.4 %collective-permute-start.3 = (f32[32,128]{1,0:T(8,128)S(1)}, f32[32,128]{1,0:T(8,128)S(1)}, u32[]{:S(2)}, u32[]{:S(2)}) collective-permute-start(f32[32,128]{1,0:T(8,128)S(1)} %get-tuple-element.30.own), channel_id=1, source_target_pairs={{0,8},{8,16},{16,24},{1,9},{9,17},{17,25},{2,10},{10,18},{18,26},{... | collective-permute-start | bytes 49160 | tf_op jit(solution)/shard_map/ppermute | solution.py:215
  78.4 14.3 %collective-permute-start.5 = (f32[32,128]{1,0:T(8,128)S(1)}, f32[32,128]{1,0:T(8,128)S(1)}, u32[]{:S(2)}, u32[]{:S(2)}) collective-permute-start(f32[32,128]{1,0:T(8,128)S(1)} %broadcast_select_fusion), channel_id=1, source_target_pairs={{16,24},{24,16},{17,25},{25,17},{18,26},{26,18},{19,27},{27,19},{2... | collective-permute-start | bytes 49160 | tf_op jit(solution)/shard_map/ppermute | solution.py:215
  96.9 10.2 %all-to-all-start = ((bf16[4,256,128]{2,1,0:T(8,128)(2,1)}), bf16[4,256,128]{2,1,0:T(8,128)(2,1)S(1)}, u32[]{:S(2)}, u32[]{:S(2)}) async-start(bf16[4,256,128]{2,1,0:T(8,128)(2,1)} %bitcast.11), calls=%async_computation | async-start | bytes 524288 | tf_op jit(solution)/shard_map/all_to_all | solution.py:301
  100.3 20.6 %collective-permute-start.6 = (bf16[4,4,4,16,1024]{4,3,2,1,0:T(8,128)(2,1)}, bf16[4,4,4,16,1024]{4,3,2,1,0:T(8,128)(2,1)}, u32[]{:S(2)}, u32[]{:S(2)}) collective-permute-start(bf16[4,4,4,16,1024]{4,3,2,1,0:T(8,128)(2,1)} %all-to-all-done.3.mine), channel_id=1, source_target_pairs={{0,1},{1,0},{2,3},{3,2},{4,5},{5,4},{6,7},{7,6},{8,9},{9,8},{10,11... | collective-permute-start | bytes 6291464 | tf_op jit(solution)/shard_map/ppermute | solution.py:215
